TPU v7x, 32 devices: a whole 2x2x4 slice. The times are simulated.
32 devices in a mesh: cell: 8 (over z, y), region: 4 (over x, core).
Axes of the slice: x: 2, y: 2, z: 4, core: 2. Of those that a mesh axis runs over, the one named last changes fastest.
Arguments:
- observed: bfloat16 [8192, 16384], P('cell', 'region'), may hold values from -0.5 to 0.5
- block_mask: int32 [1024, 128], P('cell', 'region'), may hold values 0 or 1
- plan: int32 [4], replicated, may hold values from 0 to 3, each once
- cell_factors: float32 [8192, 256], P('cell'), may hold values from -6 to 6
- region_factors: float32 [32768, 256], P(('cell', 'region')), may hold values from -6 to 6
Outputs:
- new_cells: float32 [8192, 256], P('cell')
- new_regions: float32 [32768, 256], P(('cell', 'region'))
Inputs may be any that keep to these rules, and one draw needn't show every extreme that they name: `plan`: each stored slot 0 to 3 appears once.
All inputs are finite; a program needn't handle non-finite values. No bound on the sum of `block_mask` on one device may be relied on, other than what follows from the above.
Results may differ from a plain program's by a relative error of at most 0.0056.
Values sent between devices are 32-bit elements; how exact they have to be, the bound alone decides.
No kernel may reach another device: no remote copies, remote signals or barrier semaphores. Data moves between devices by JAX's collectives and lax.ppermute only.
A program may use at most 64 MiB of HBM per device.

v0:
```python
import math
import jax
import jax.numpy as jnp
from jax import lax
from jax.sharding import PartitionSpec as P

STRATA = 4
beta_mom = 0.9


def shifted(value, axis, steps):
    count = lax.axis_size(axis)
    pairs = [(source, (source + steps) % count) for source in range(count)]
    return lax.ppermute(value, axis, pairs)


def body(observed, block_mask, plan, cell_factors, region_factors):
    n_region = lax.axis_size("region")
    cell_rows = cell_factors.shape[0]
    block_rows = region_factors.shape[0]
    total_cols = n_region * block_rows
    scale_pred = 0.5 / math.sqrt(total_cols)
    rate_region = total_cols / cell_rows
    cells_now = cell_factors
    regions_now = region_factors
    momentum = jnp.zeros_like(cell_factors)
    for section in range(STRATA):
        slot_index = plan[section]
        data_block = lax.dynamic_slice_in_dim(observed, slot_index * block_rows, block_rows, 1)
        mask_block = lax.dynamic_slice_in_dim(
            block_mask, slot_index * (block_rows // 128), block_rows // 128, 1
        )
        expanded = jnp.broadcast_to(
            mask_block[:, None, :, None], (cell_rows // 8, 8, block_rows // 128, 128)
        )
        expanded = expanded.reshape(cell_rows, block_rows).astype(jnp.float32)
        cell_bf = cells_now.astype(jnp.bfloat16)
        region_bf = regions_now.astype(jnp.bfloat16)
        predicted = lax.dot_general(
            cell_bf, region_bf, (((1,), (1,)), ((), ())), preferred_element_type=jnp.float32
        )
        resid = (expanded * (scale_pred * predicted - data_block.astype(jnp.float32))).astype(
            jnp.bfloat16
        )
        grad_cell = scale_pred * jnp.dot(resid, region_bf, preferred_element_type=jnp.float32)
        grad_region = scale_pred * lax.dot_general(
            resid, cell_bf, (((0,), (0,)), ((), ())), preferred_element_type=jnp.float32
        )
        regions_now = regions_now - rate_region * grad_region
        grad_total = lax.psum(grad_cell, "region")
        momentum = beta_mom * momentum + grad_total
        cells_now = cells_now - momentum
        if section + 1 < STRATA:
            regions_now = shifted(regions_now, "cell", -1)
    regions_now = shifted(regions_now, "cell", STRATA - 1)
    return (cells_now, regions_now)


def solution(mesh):
    in_specs = (
        P("cell", "region"),
        P("cell", "region"),
        P(),
        P("cell", None),
        P(("cell", "region"), None),
    )
    out_specs = (P("cell", None), P(("cell", "region"), None))
    return jax.shard_map(body, mesh=mesh, in_specs=in_specs, out_specs=out_specs, check_vma=False)
```

profile of v0, /device:TPU:0, one launch (start us, length us, event | category | flops | bytes accessed | tf_op | source)
XLA Modules:
  0.0 219.6 jit_solution(5115374856449592697)
XLA Ops:
  7.2 0.0 all-reduce.5.cloned.1.call-start
  7.2 1.5 fusion.26
  12.0 0.7 dynamic-slice_convert_fusion
  12.7 0.1 copy.7
  12.8 0.0 copy-start.1
  12.8 0.0 copy-start.2
  12.8 3.2 %fusion.3 = bf16[1024,1024]{1,0:T(8,128)(2,1)S(1)} fusion(bf16[1024,4096]{1,0:T(8,128)(2,1)} %param.5, s32[]{:T(128)S(6)} %select_n.25, f32[128,8]{1,0:T(8,128)S(1)} %copy.7, f32[1024,256]{1,0:T(8,128)} %param.9, f32[1024,256]{1,0:T(8,128)} %param.8), kind=kOutput, calls=%fused_computation.7 | convolution fusion | flops 542638080 | bytes 6295556 | tf_op jit(solution)/shard_map/dot_general | solution.py:39
  16.0 0.0 copy-done.1
  16.0 0.0 copy-done.2
  16.0 1.7 fusion.7
  17.8 6.0 %collective-permute-start = (f32[1024,256]{1,0:T(8,128)}, f32[1024,256]{1,0:T(8,128)S(1)}, u32[]{:S(2)}, u32[]{:S(2)}) collective-permute-start(f32[1024,256]{1,0:T(8,128)} %fusion.7), channel_id=1, source_target_pairs={{0,28},{4,0},{8,4},{12,8},{16,12},{20,16},{24,20},{28,24},{1,29},{... | collective-permute-start | bytes 3145736 | tf_op jit(solution)/shard_map/ppermute | solution.py:14
  23.8 1.7 convolution_multiply_fusion.7
  25.5 0.0 all-reduce.5.cloned.1.call-update
  25.5 0.0 all-reduce.7.cloned.1.call-start
  26.2 0.1 copy.8
  26.3 32.9 %all-reduce.5.cloned.1.call-done = f32[1024,256]{1,0:T(8,128)} async-done(((f32[1024,256]{1,0:T(8,128)}), f32[1024,256]{1,0:T(8,128)}) %all-reduce.5.cloned.1.call-update) | async-done | bytes 1048592 | tf_op jit(solution)/shard_map/psum | solution.py:50
  59.2 1.4 sub.37
  60.5 0.0 collective-permute-done
  60.6 3.3 %fusion.2 = bf16[1024,1024]{1,0:T(8,128)(2,1)S(1)} fusion(bf16[1024,4096]{1,0:T(8,128)(2,1)} %param.5, s32[]{:T(128)S(6)} %select_n.27, f32[128,8]{1,0:T(8,128)S(1)} %copy.8, f32[1024,256]{1,0:T(8,128)S(1)} %collective-permute-done, f32[1024,256]{1,0:T(8,128)S(1)} %sub.37), kind=kOutput, calls=%fused_computation.5 | convolution fusion | flops 542638080 | bytes 6295556 | tf_op jit(solution)/shard_map/dot_general | solution.py:39
  63.8 1.8 fusion.6
  65.6 0.0 copy-start
  65.6 4.2 %collective-permute-start.1 = (f32[1024,256]{1,0:T(8,128)}, f32[1024,256]{1,0:T(8,128)}, u32[]{:S(2)}, u32[]{:S(2)}) collective-permute-start(f32[1024,256]{1,0:T(8,128)} %fusion.6), channel_id=1, source_target_pairs={{0,28},{4,0},{8,4},{12,8},{16,12},{20,16},{24,20},{28,24},{1,29},{... | collective-permute-start | bytes 3145736 | tf_op jit(solution)/shard_map/ppermute | solution.py:14
  69.8 1.7 convolution_multiply_fusion.5
  71.5 0.0 all-reduce.7.cloned.1.call-update
  71.5 0.0 all-reduce.9.cloned.1.call-start
  72.3 0.1 copy.9
  72.4 32.4 %all-reduce.7.cloned.1.call-done = f32[1024,256]{1,0:T(8,128)} async-done(((f32[1024,256]{1,0:T(8,128)}), f32[1024,256]{1,0:T(8,128)}) %all-reduce.7.cloned.1.call-update) | async-done | bytes 1048592 | tf_op jit(solution)/shard_map/psum | solution.py:50
  104.8 0.0 copy-done
  104.8 1.4 fusion.8
  106.2 0.0 collective-permute-done.1
  106.2 3.6 %fusion.1 = bf16[1024,1024]{1,0:T(8,128)(2,1)S(1)} fusion(bf16[1024,4096]{1,0:T(8,128)(2,1)} %param.5, s32[]{:T(128)S(6)} %select_n.29, f32[128,8]{1,0:T(8,128)S(1)} %copy.9, f32[1024,256]{1,0:T(8,128)} %collective-permute-done.1, f32[1024,256]{1,0:T(8,128)S(1)} %fusion.8), kind=kOutput, calls=%fused_computation.3 | convolution fusion | flops 542638080 | bytes 6295556 | tf_op jit(solution)/shard_map/dot_general | solution.py:39
  109.8 3.0 %fusion.5 = f32[1024,256]{1,0:T(8,128)} fusion(f32[1024,256]{1,0:T(8,128)} %collective-permute-done.1, bf16[1024,1024]{1,0:T(8,128)(2,1)S(1)} %fusion.1, f32[1024,256]{1,0:T(8,128)S(1)} %fusion.8), kind=kOutput, calls=%fused_computation.12 | convolution fusion | flops 537657344 | bytes 5242880 | tf_op jit(solution)/shard_map/dot_general | solution.py:46
  112.8 4.2 %collective-permute-start.2 = (f32[1024,256]{1,0:T(8,128)}, f32[1024,256]{1,0:T(8,128)}, u32[]{:S(2)}, u32[]{:S(2)}) collective-permute-start(f32[1024,256]{1,0:T(8,128)} %fusion.5), channel_id=1, source_target_pairs={{0,28},{4,0},{8,4},{12,8},{16,12},{20,16},{24,20},{28,24},{1,29},{... | collective-permute-start | bytes 3145736 | tf_op jit(solution)/shard_map/ppermute | solution.py:14
  117.0 2.9 %convolution_multiply_fusion.3 = f32[1024,256]{1,0:T(8,128)} fusion(bf16[1024,1024]{1,0:T(8,128)(2,1)S(1)} %fusion.1, f32[1024,256]{1,0:T(8,128)} %collective-permute-done.1), kind=kOutput, calls=%fused_computation.13 | convolution fusion | flops 537395200 | bytes 4194304 | tf_op jit(solution)/shard_map/dot_general | solution.py:45
  119.9 0.0 all-reduce.9.cloned.1.call-update
  120.0 0.0 all-reduce.11.cloned.1.call-start
  120.7 0.1 copy.10
  120.8 32.4 %all-reduce.9.cloned.1.call-done = f32[1024,256]{1,0:T(8,128)} async-done(((f32[1024,256]{1,0:T(8,128)}), f32[1024,256]{1,0:T(8,128)}) %all-reduce.9.cloned.1.call-update) | async-done | bytes 1048592 | tf_op jit(solution)/shard_map/psum | solution.py:50
  153.2 1.8 fusion.25
  155.0 0.0 collective-permute-done.2
  155.0 3.6 %fusion = bf16[1024,1024]{1,0:T(8,128)(2,1)S(1)} fusion(bf16[1024,4096]{1,0:T(8,128)(2,1)} %param.5, s32[]{:T(128)S(6)} %select_n.31, f32[128,8]{1,0:T(8,128)S(1)} %copy.10, f32[1024,256]{1,0:T(8,128)} %collective-permute-done.2, f32[1024,256]{1,0:T(8,128)S(1)} %fusion.25), kind=kOutput, calls=%fused_computation.1 | convolution fusion | flops 542638080 | bytes 6295556 | tf_op jit(solution)/shard_map/dot_general | solution.py:39
  158.6 3.0 %fusion.4 = f32[1024,256]{1,0:T(8,128)} fusion(f32[1024,256]{1,0:T(8,128)} %collective-permute-done.2, bf16[1024,1024]{1,0:T(8,128)(2,1)S(1)} %fusion, f32[1024,256]{1,0:T(8,128)S(1)} %fusion.25), kind=kOutput, calls=%fused_computation.9 | convolution fusion | flops 537657344 | bytes 5242880 | tf_op jit(solution)/shard_map/dot_general | solution.py:46
  161.6 0.0 copy-start.3
  161.6 2.4 %collective-permute-start.3 = (f32[1024,256]{1,0:T(8,128)}, f32[1024,256]{1,0:T(8,128)}, u32[]{:S(2)}, u32[]{:S(2)}) collective-permute-start(f32[1024,256]{1,0:T(8,128)} %fusion.4), channel_id=1, source_target_pairs={{0,12},{4,16},{8,20},{12,24},{16,28},{20,0},{24,4},{28,8},{1,13},{... | collective-permute-start | bytes 3145736 | tf_op jit(solution)/shard_map/ppermute | solution.py:14
  164.0 2.9 %convolution_multiply_fusion.1 = f32[1024,256]{1,0:T(8,128)} fusion(bf16[1024,1024]{1,0:T(8,128)(2,1)S(1)} %fusion, f32[1024,256]{1,0:T(8,128)} %collective-permute-done.2), kind=kOutput, calls=%fused_computation.10 | convolution fusion | flops 537395200 | bytes 4194304 | tf_op jit(solution)/shard_map/dot_general | solution.py:45
  166.9 0.0 all-reduce.11.cloned.1.call-update
  167.0 35.3 %all-reduce.11.cloned.1.call-done = f32[1024,256]{1,0:T(8,128)} async-done(((f32[1024,256]{1,0:T(8,128)}), f32[1024,256]{1,0:T(8,128)}) %all-reduce.11.cloned.1.call-update) | async-done | bytes 1048592 | tf_op jit(solution)/shard_map/psum | solution.py:50
  202.3 0.0 copy-done.3
  202.3 2.8 %add_subtract_fusion = f32[1024,256]{1,0:T(8,128)} fusion(f32[1024,256]{1,0:T(8,128)S(1)} %fusion.25, f32[1024,256]{1,0:T(8,128)} %all-reduce.11.cloned.1.call-done, f32[1024,256]{1,0:T(8,128)} %all-reduce.9.cloned.1.call-done, f32[1024,256]{1,0:T(8,128)S(1)} %copy-done.3, f32[1024,256]{1,0:T(8,128)S(1)} %copy-done), kind=kLoop, calls=%fused_computation.20 | loop fusion | flops 1835008 | bytes 6291456 | tf_op jit(solution)/shard_map/sub | solution.py:52
  205.1 5.6 %collective-permute-done.3 = f32[1024,256]{1,0:T(8,128)} collective-permute-done((f32[1024,256]{1,0:T(8,128)}, f32[1024,256]{1,0:T(8,128)}, u32[]{:S(2)}, u32[]{:S(2)}) %collective-permute-start.3) | collective-permute-done | bytes 1048608 | tf_op jit(solution)/shard_map/ppermute | solution.py:14
  210.8 2.3 %copy.16 = f32[1024,256]{1,0:T(8,128)} copy(f32[1024,256]{1,0:T(8,128)} %collective-permute-done.3) | data formatting | bytes 2097152
Async XLA Ops:
  7.2 52.0 %all-reduce.5.cloned.1.call-start = ((), (), s32[]{:S(2)}) async-start(), calls=%async_computation | async-start | bytes 2097152 | tf_op jit(solution)/shard_map/psum | solution.py:50
  12.8 3.2 %copy-start.1 = (f32[1024,256]{1,0:T(8,128)S(1)}, f32[1024,256]{1,0:T(8,128)}, u32[]{:S(2)}) copy-start(f32[1024,256]{1,0:T(8,128)} %param.9) | copy-start | bytes 3145732
  12.8 3.2 %copy-start.2 = (f32[1024,256]{1,0:T(8,128)S(1)}, f32[1024,256]{1,0:T(8,128)}, u32[]{:S(2)}) copy-start(f32[1024,256]{1,0:T(8,128)} %param.8) | copy-start | bytes 3145732
  17.8 42.8 %collective-permute-start = (f32[1024,256]{1,0:T(8,128)}, f32[1024,256]{1,0:T(8,128)S(1)}, u32[]{:S(2)}, u32[]{:S(2)}) collective-permute-start(f32[1024,256]{1,0:T(8,128)} %fusion.7), channel_id=1, source_target_pairs={{0,28},{4,0},{8,4},{12,8},{16,12},{20,16},{24,20},{28,24},{1,29},{... | collective-permute-start | bytes 3145736 | tf_op jit(solution)/shard_map/ppermute | solution.py:14
  25.5 79.2 %all-reduce.7.cloned.1.call-start = ((), (), s32[]{:S(2)}) async-start(), calls=%async_computation.1 | async-start | bytes 2097152 | tf_op jit(solution)/shard_map/psum | solution.py:50
  65.6 39.2 %copy-start = (f32[1024,256]{1,0:T(8,128)S(1)}, f32[1024,256]{1,0:T(8,128)}, u32[]{:S(2)}) copy-start(f32[1024,256]{1,0:T(8,128)} %all-reduce.5.cloned.1.call-done) | copy-start | bytes 3145732
  65.6 40.6 %collective-permute-start.1 = (f32[1024,256]{1,0:T(8,128)}, f32[1024,256]{1,0:T(8,128)}, u32[]{:S(2)}, u32[]{:S(2)}) collective-permute-start(f32[1024,256]{1,0:T(8,128)} %fusion.6), channel_id=1, source_target_pairs={{0,28},{4,0},{8,4},{12,8},{16,12},{20,16},{24,20},{28,24},{1,29},{... | collective-permute-start | bytes 3145736 | tf_op jit(solution)/shard_map/ppermute | solution.py:14
  71.5 81.6 %all-reduce.9.cloned.1.call-start = ((), (), s32[]{:S(2)}) async-start(), calls=%async_computation.2 | async-start | bytes 2097152 | tf_op jit(solution)/shard_map/psum | solution.py:50
  112.8 42.2 %collective-permute-start.2 = (f32[1024,256]{1,0:T(8,128)}, f32[1024,256]{1,0:T(8,128)}, u32[]{:S(2)}, u32[]{:S(2)}) collective-permute-start(f32[1024,256]{1,0:T(8,128)} %fusion.5), channel_id=1, source_target_pairs={{0,28},{4,0},{8,4},{12,8},{16,12},{20,16},{24,20},{28,24},{1,29},{... | collective-permute-start | bytes 3145736 | tf_op jit(solution)/shard_map/ppermute | solution.py:14
  120.0 82.3 %all-reduce.11.cloned.1.call-start = ((), (), s32[]{:S(2)}) async-start(), calls=%async_computation.3 | async-start | bytes 2097152 | tf_op jit(solution)/shard_map/psum | solution.py:50
  161.6 40.7 %copy-start.3 = (f32[1024,256]{1,0:T(8,128)S(1)}, f32[1024,256]{1,0:T(8,128)}, u32[]{:S(2)}) copy-start(f32[1024,256]{1,0:T(8,128)} %all-reduce.7.cloned.1.call-done) | copy-start | bytes 3145732
  161.6 49.1 %collective-permute-start.3 = (f32[1024,256]{1,0:T(8,128)}, f32[1024,256]{1,0:T(8,128)}, u32[]{:S(2)}, u32[]{:S(2)}) collective-permute-start(f32[1024,256]{1,0:T(8,128)} %fusion.4), channel_id=1, source_target_pairs={{0,12},{4,16},{8,20},{12,24},{16,28},{20,0},{24,4},{28,8},{1,13},{... | collective-permute-start | bytes 3145736 | tf_op jit(solution)/shard_map/ppermute | solution.py:14
Sparse Core Ops, SparseCore 0:
  25.7 33.4 all-reduce.4
  71.7 33.0 all-reduce.6
  120.1 33.0 all-reduce.8
  167.1 35.1 all-reduce.10
where the time goes:
time: 220 us
  waiting for transfers between devices  139 us (63%)
  matrix products  32.3 us (15%)
  between operations  19.2 us (9%)
  starting transfers between devices  17.1 us (8%)
  other arithmetic  8.19 us (4%)
  local copies, waits for them, and re-layouts  4.15 us (2%)
    psum x4, waiting for transfers between devices, body(): grad_total = lax.psum(grad_cell, 'region')  133 us
    ppermute x4, starting transfers between devices, shifted(): return lax.ppermute(value, axis, pairs)  16.9 us
    dot_general x4, matrix products, body(): lax.dot_general(cell_bf, region_bf, (((1,), (1,)), ((), ())), preferred_e...  13.6 us
    dot_general x4, matrix products, body(): lax.dot_general(resid, cell_bf, (((0,), (0,)), ((), ())), preferred_eleme...  9.47 us
    dot_general x4, matrix products, body(): jnp.dot(resid, region_bf, preferred_element_type=jnp.float32)  9.23 us
    sub x4, other arithmetic, body(): cells_now = cells_now - momentum  7.45 us
    ppermute x4, waiting for transfers between devices, shifted(): return lax.ppermute(value, axis, pairs)  5.62 us
  transfers between devices with their start and end apart: 8, of which 5 were waited for; matrix products, arithmetic and copies ran while one was open for 8% of the time, Pallas kernels for 0%

commit v1 on v0

--- a/solution.py
+++ b/solution.py
@@ -47,7 +47,11 @@
             resid, cell_bf, (((0,), (0,)), ((), ())), preferred_element_type=jnp.float32
         )
         regions_now = regions_now - rate_region * grad_region
-        grad_total = lax.psum(grad_cell, "region")
+        grad_total = grad_cell
+        for hop in (1, 2):
+            grad_total = grad_total + lax.ppermute(
+                grad_total, "region", [(dev, dev ^ hop) for dev in range(4)]
+            )
         momentum = beta_mom * momentum + grad_total
         cells_now = cells_now - momentum
         if section + 1 < STRATA:

time: 220 us -> 181 us (0.82)
  waiting for transfers between devices: 139 us -> 115 us
  between operations: 19.2 us -> 5.68 us
  matrix products: 32.3 us -> 21.8 us
  other arithmetic: 8.19 us -> 13.5 us
  starting transfers between devices: 17.1 us -> 21.1 us
    psum x4 -> x0, waiting for transfers between devices: 133 us -> none  [body(): grad_total = lax.psum(grad_cell, 'region')]
    ppermute x0 -> x8, waiting for transfers between devices: none -> 59.9 us  [body(): lax.ppermute(grad_total, 'region', [(dev, dev ^ hop) for dev in range(4)])]
    ppermute x4, waiting for transfers between devices: 5.62 us -> 55.6 us  [shifted(): return lax.ppermute(value, axis, pairs)]
    dot_general x4, matrix products: 9.23 us -> 2.9 us  [body(): jnp.dot(resid, region_bf, preferred_element_type=jnp.float32)]
    ppermute x0 -> x8, starting transfers between devices: none -> 6.31 us  [body(): lax.ppermute(grad_total, 'region', [(dev, dev ^ hop) for dev in range(4)])]
    dot_general x4, matrix products: 9.47 us -> 6.05 us  [body(): lax.dot_general(resid, cell_bf, (((0,), (0,)), ((), ())), preferred_eleme...]
    sub x4, other arithmetic: 7.45 us -> 10.3 us  [body(): cells_now = cells_now - momentum]
    add x0 -> x4, other arithmetic: none -> 2.48 us  [body(): grad_total + lax.ppermute(grad_total, 'region', [(dev, dev ^ hop) for dev...]
  transfers between devices with their start and end apart: 8 -> 12, of which waited for: 5 -> 11; matrix products, arithmetic and copies ran while one was open for 8% -> 8% of each run, Pallas kernels for 0% -> 0%
where the time goes in v1:
time: 181 us; the launch traced here: 180 us
  waiting for transfers between devices  115 us (64%)
  matrix products  21.8 us (12%)
  starting transfers between devices  21.1 us (12%)
  other arithmetic  13.5 us (7%)
  between operations  5.68 us (3%)
  local copies, waits for them, and re-layouts  2.87 us (2%)
    ppermute x8, waiting for transfers between devices, body(): lax.ppermute(grad_total, 'region', [(dev, dev ^ hop) for dev in range(4)])  59.9 us
    ppermute x4, waiting for transfers between devices, shifted(): return lax.ppermute(value, axis, pairs)  55.6 us
    ppermute x4, starting transfers between devices, shifted(): return lax.ppermute(value, axis, pairs)  14.8 us
    dot_general x4, matrix products, body(): lax.dot_general(cell_bf, region_bf, (((1,), (1,)), ((), ())), preferred_e...  12.8 us
    sub x4, other arithmetic, body(): cells_now = cells_now - momentum  10.3 us
    ppermute x8, starting transfers between devices, body(): lax.ppermute(grad_total, 'region', [(dev, dev ^ hop) for dev in range(4)])  6.31 us
    dot_general x4, matrix products, body(): lax.dot_general(resid, cell_bf, (((0,), (0,)), ((), ())), preferred_eleme...  6.05 us
  transfers between devices with their start and end apart: 12, of which 11 were waited for; matrix products, arithmetic and copies ran while one was open for 8% of the time, Pallas kernels for 0%

profile of v1, /device:TPU:0, one launch (start us, length us, event | category | flops | bytes accessed | tf_op | source)
XLA Modules:
  0.0 180.4 jit_solution(12425229545233691372)
XLA Ops:
  0.6 1.5 fusion.26
  5.2 0.7 dynamic-slice_convert_fusion
  5.9 0.1 copy.7
  6.0 0.0 copy-start
  6.0 3.1 %fusion.3 = bf16[1024,1024]{1,0:T(8,128)(2,1)S(1)} fusion(bf16[1024,4096]{1,0:T(8,128)(2,1)} %param.5, s32[]{:T(128)S(6)} %select_n.25, f32[128,8]{1,0:T(8,128)S(1)} %copy.7, f32[1024,256]{1,0:T(8,128)} %param.9, f32[1024,256]{1,0:T(8,128)} %param.8), kind=kOutput, calls=%fused_computation.7 | convolution fusion | flops 542638080 | bytes 6295556 | tf_op jit(solution)/shard_map/dot_general | solution.py:39
  9.2 0.0 copy-done
  9.2 0.7 convolution_multiply_fusion.7
  9.9 0.0 copy-start.2
  9.9 0.6 collective-permute-start
  10.5 2.3 %collective-permute-done = f32[1024,256]{1,0:T(8,128)S(1)} collective-permute-done((f32[1024,256]{1,0:T(8,128)S(1)}, f32[1024,256]{1,0:T(8,128)S(1)}, u32[]{:S(2)}, u32[]{:S(2)}) %collective-permute-start) | collective-permute-done | bytes 1048608 | tf_op jit(solution)/shard_map/ppermute | solution.py:52
  12.8 0.1 add.59
  12.9 0.0 copy-start.3
  12.9 2.9 %collective-permute-start.1 = (f32[1024,256]{1,0:T(8,128)S(1)}, f32[1024,256]{1,0:T(8,128)}, u32[]{:S(2)}, u32[]{:S(2)}) collective-permute-start(f32[1024,256]{1,0:T(8,128)S(1)} %add.59), channel_id=1, source_target_pairs={{0,2},{1,3},{2,0},{3,1},{4,6},{5,7},{6,4},{7,5},{8,10},{9,11},{10,... | collective-permute-start | bytes 3145736 | tf_op jit(solution)/shard_map/ppermute | solution.py:52
  15.8 0.0 copy-done.2
  15.8 1.7 fusion.7
  17.6 0.0 copy-done.3
  17.6 4.6 %collective-permute-start.2 = (f32[1024,256]{1,0:T(8,128)}, f32[1024,256]{1,0:T(8,128)S(1)}, u32[]{:S(2)}, u32[]{:S(2)}) collective-permute-start(f32[1024,256]{1,0:T(8,128)} %fusion.7), channel_id=1, source_target_pairs={{0,28},{4,0},{8,4},{12,8},{16,12},{20,16},{24,20},{28,24},{1,29},{... | collective-permute-start | bytes 3145736 | tf_op jit(solution)/shard_map/ppermute | solution.py:14
  22.7 0.1 copy.8
  22.8 16.6 %collective-permute-done.1 = f32[1024,256]{1,0:T(8,128)} collective-permute-done((f32[1024,256]{1,0:T(8,128)S(1)}, f32[1024,256]{1,0:T(8,128)}, u32[]{:S(2)}, u32[]{:S(2)}) %collective-permute-start.1) | collective-permute-done | bytes 1048608 | tf_op jit(solution)/shard_map/ppermute | solution.py:52
  39.4 1.7 add_subtract_fusion.1
  41.1 3.7 %collective-permute-done.2 = f32[1024,256]{1,0:T(8,128)S(1)} collective-permute-done((f32[1024,256]{1,0:T(8,128)}, f32[1024,256]{1,0:T(8,128)S(1)}, u32[]{:S(2)}, u32[]{:S(2)}) %collective-permute-start.2) | collective-permute-done | bytes 1048608 | tf_op jit(solution)/shard_map/ppermute | solution.py:14
  44.9 3.2 %fusion.2 = bf16[1024,1024]{1,0:T(8,128)(2,1)S(1)} fusion(bf16[1024,4096]{1,0:T(8,128)(2,1)} %param.5, s32[]{:T(128)S(6)} %select_n.27, f32[128,8]{1,0:T(8,128)S(1)} %copy.8, f32[1024,256]{1,0:T(8,128)S(1)} %collective-permute-done.2, f32[1024,256]{1,0:T(8,128)S(1)} %add_subtract_fusion.1), kind=kOutput, calls=%fused_computation.5 | convolution fusion | flops 542638080 | bytes 6295556 | tf_op jit(solution)/shard_map/dot_general | solution.py:39
  48.1 0.7 convolution_multiply_fusion.5
  48.9 0.1 collective-permute-start.3
  48.9 2.6 %collective-permute-done.3 = f32[1024,256]{1,0:T(8,128)S(1)} collective-permute-done((f32[1024,256]{1,0:T(8,128)S(1)}, f32[1024,256]{1,0:T(8,128)S(1)}, u32[]{:S(2)}, u32[]{:S(2)}) %collective-permute-start.3) | collective-permute-done | bytes 1048608 | tf_op jit(solution)/shard_map/ppermute | solution.py:52
  51.6 1.1 add.63
  52.7 0.5 collective-permute-start.4
  53.2 1.8 fusion.6
  55.0 5.1 %collective-permute-start.5 = (f32[1024,256]{1,0:T(8,128)}, f32[1024,256]{1,0:T(8,128)S(1)}, u32[]{:S(2)}, u32[]{:S(2)}) collective-permute-start(f32[1024,256]{1,0:T(8,128)} %fusion.6), channel_id=1, source_target_pairs={{0,28},{4,0},{8,4},{12,8},{16,12},{20,16},{24,20},{28,24},{1,29},{... | collective-permute-start | bytes 3145736 | tf_op jit(solution)/shard_map/ppermute | solution.py:14
  60.6 0.1 copy.9
  60.7 17.5 %collective-permute-done.4 = f32[1024,256]{1,0:T(8,128)} collective-permute-done((f32[1024,256]{1,0:T(8,128)}, f32[1024,256]{1,0:T(8,128)}, u32[]{:S(2)}, u32[]{:S(2)}) %collective-permute-start.4) | collective-permute-done | bytes 1048608 | tf_op jit(solution)/shard_map/ppermute | solution.py:52
  78.2 3.5 %fusion.25 = (f32[1024,256]{1,0:T(8,128)S(1)}, f32[1024,256]{1,0:T(8,128)}) fusion(f32[1024,256]{1,0:T(8,128)S(1)} %add_subtract_fusion.1, f32[1024,256]{1,0:T(8,128)} %add.63, f32[1024,256]{1,0:T(8,128)} %collective-permute-done.4, f32[1024,256]{1,0:T(8,128)} %copy-done.3, f32[1024,256]{1,0:T(8,128)} %collective-permute-done.1), kind=kLoop, calls=%fused_computation.45 | loop fusion | flops 1310720 | bytes 7340032 | tf_op jit(solution)/shard_map/sub | solution.py:56
  81.7 1.1 collective-permute-done.5
  82.8 3.2 %fusion.1 = bf16[1024,1024]{1,0:T(8,128)(2,1)S(1)} fusion(bf16[1024,4096]{1,0:T(8,128)(2,1)} %param.5, s32[]{:T(128)S(6)} %select_n.29, f32[128,8]{1,0:T(8,128)S(1)} %copy.9, f32[1024,256]{1,0:T(8,128)S(1)} %collective-permute-done.5, f32[1024,256]{1,0:T(8,128)S(1)} %get-tuple-element.2), kind=kOutput, calls=%fused_computation.3 | convolution fusion | flops 542638080 | bytes 6295556 | tf_op jit(solution)/shard_map/dot_general | solution.py:39
  86.1 0.7 convolution_multiply_fusion.3
  86.8 0.1 collective-permute-start.6
  86.9 2.6 %collective-permute-done.6 = f32[1024,256]{1,0:T(8,128)S(1)} collective-permute-done((f32[1024,256]{1,0:T(8,128)S(1)}, f32[1024,256]{1,0:T(8,128)S(1)}, u32[]{:S(2)}, u32[]{:S(2)}) %collective-permute-start.6) | collective-permute-done | bytes 1048608 | tf_op jit(solution)/shard_map/ppermute | solution.py:52
  89.5 1.1 add.68
  90.6 1.5 collective-permute-start.7
  92.1 1.8 fusion.5
  93.9 5.1 %collective-permute-start.8 = (f32[1024,256]{1,0:T(8,128)}, f32[1024,256]{1,0:T(8,128)S(1)}, u32[]{:S(2)}, u32[]{:S(2)}) collective-permute-start(f32[1024,256]{1,0:T(8,128)} %fusion.5), channel_id=1, source_target_pairs={{0,28},{4,0},{8,4},{12,8},{16,12},{20,16},{24,20},{28,24},{1,29},{... | collective-permute-start | bytes 3145736 | tf_op jit(solution)/shard_map/ppermute | solution.py:14
  99.6 0.1 copy.10
  99.7 16.4 %collective-permute-done.7 = f32[1024,256]{1,0:T(8,128)} collective-permute-done((f32[1024,256]{1,0:T(8,128)}, f32[1024,256]{1,0:T(8,128)}, u32[]{:S(2)}, u32[]{:S(2)}) %collective-permute-start.7) | collective-permute-done | bytes 1048608 | tf_op jit(solution)/shard_map/ppermute | solution.py:52
  116.1 2.1 %fusion.24 = f32[1024,256]{1,0:T(8,128)S(1)} fusion(f32[1024,256]{1,0:T(8,128)S(1)} %get-tuple-element.2, f32[1024,256]{1,0:T(8,128)} %add.68, f32[1024,256]{1,0:T(8,128)} %collective-permute-done.7, f32[1024,256]{1,0:T(8,128)} %get-tuple-element.3), kind=kLoop, calls=%fused_computation.44 | loop fusion | flops 1048576 | bytes 5242880 | tf_op jit(solution)/shard_map/sub | solution.py:56
  118.3 3.4 %collective-permute-done.8 = f32[1024,256]{1,0:T(8,128)S(1)} collective-permute-done((f32[1024,256]{1,0:T(8,128)}, f32[1024,256]{1,0:T(8,128)S(1)}, u32[]{:S(2)}, u32[]{:S(2)}) %collective-permute-start.8) | collective-permute-done | bytes 1048608 | tf_op jit(solution)/shard_map/ppermute | solution.py:14
  121.7 3.2 %fusion = bf16[1024,1024]{1,0:T(8,128)(2,1)S(1)} fusion(bf16[1024,4096]{1,0:T(8,128)(2,1)} %param.5, s32[]{:T(128)S(6)} %select_n.31, f32[128,8]{1,0:T(8,128)S(1)} %copy.10, f32[1024,256]{1,0:T(8,128)S(1)} %collective-permute-done.8, f32[1024,256]{1,0:T(8,128)S(1)} %fusion.24), kind=kOutput, calls=%fused_computation.1 | convolution fusion | flops 542638080 | bytes 6295556 | tf_op jit(solution)/shard_map/dot_general | solution.py:39
  125.0 0.7 convolution_multiply_fusion.1
  125.7 0.1 collective-permute-start.9
  125.8 0.8 fusion.4
  126.6 0.0 copy-start.1
  126.6 0.1 collective-permute-start.11
  126.7 1.8 collective-permute-done.9
  128.4 0.1 add.73
  128.6 0.6 collective-permute-start.10
  129.2 47.3 %collective-permute-done.11 = f32[1024,256]{1,0:T(8,128)S(1)} collective-permute-done((f32[1024,256]{1,0:T(8,128)S(1)}, f32[1024,256]{1,0:T(8,128)S(1)}, u32[]{:S(2)}, u32[]{:S(2)}) %collective-permute-start.11) | collective-permute-done | bytes 1048608 | tf_op jit(solution)/shard_map/ppermute | solution.py:14
  176.5 0.0 collective-permute-done.10
  176.5 0.0 copy-done.1
  176.5 2.9 %add_subtract_fusion = f32[1024,256]{1,0:T(8,128)} fusion(f32[1024,256]{1,0:T(8,128)S(1)} %fusion.24, f32[1024,256]{1,0:T(8,128)S(1)} %add.73, f32[1024,256]{1,0:T(8,128)S(1)} %collective-permute-done.10, f32[1024,256]{1,0:T(8,128)} %add.68, f32[1024,256]{1,0:T(8,128)} %collective-permute-done.7, f32[1024,256]{1,0:T(8,128)S(1)} %copy-done.1), kind=kLoop, calls=%fused_computation.20 | loop fusion | flops 1835008 | bytes 7340032 | tf_op jit(solution)/shard_map/sub | solution.py:56
  179.4 1.0 copy.12
Async XLA Ops:
  6.0 3.1 %copy-start = (f32[1024,256]{1,0:T(8,128)S(1)}, f32[1024,256]{1,0:T(8,128)}, u32[]{:S(2)}) copy-start(f32[1024,256]{1,0:T(8,128)} %param.9) | copy-start | bytes 3145732
  9.9 5.9 %copy-start.2 = (f32[1024,256]{1,0:T(8,128)S(1)}, f32[1024,256]{1,0:T(8,128)}, u32[]{:S(2)}) copy-start(f32[1024,256]{1,0:T(8,128)} %param.8) | copy-start | bytes 3145732
  9.9 2.8 %collective-permute-start = (f32[1024,256]{1,0:T(8,128)S(1)}, f32[1024,256]{1,0:T(8,128)S(1)}, u32[]{:S(2)}, u32[]{:S(2)}) collective-permute-start(f32[1024,256]{1,0:T(8,128)S(1)} %convolution_multiply_fusion.7), channel_id=1, source_target_pairs={{0,1},{1,0},{2,3},{3,2},{4,5},{5,4},{6,7},{7,6},{8,9},{9,8},{10,11... | collective-permute-start | bytes 3145736 | tf_op jit(solution)/shard_map/ppermute | solution.py:52
  12.9 4.7 %copy-start.3 = (f32[1024,256]{1,0:T(8,128)}, f32[1024,256]{1,0:T(8,128)S(1)}, u32[]{:S(2)}) copy-start(f32[1024,256]{1,0:T(8,128)S(1)} %add.59) | copy-start | bytes 3145732
  12.9 26.5 %collective-permute-start.1 = (f32[1024,256]{1,0:T(8,128)S(1)}, f32[1024,256]{1,0:T(8,128)}, u32[]{:S(2)}, u32[]{:S(2)}) collective-permute-start(f32[1024,256]{1,0:T(8,128)S(1)} %add.59), channel_id=1, source_target_pairs={{0,2},{1,3},{2,0},{3,1},{4,6},{5,7},{6,4},{7,5},{8,10},{9,11},{10,... | collective-permute-start | bytes 3145736 | tf_op jit(solution)/shard_map/ppermute | solution.py:52
  17.6 27.3 %collective-permute-start.2 = (f32[1024,256]{1,0:T(8,128)}, f32[1024,256]{1,0:T(8,128)S(1)}, u32[]{:S(2)}, u32[]{:S(2)}) collective-permute-start(f32[1024,256]{1,0:T(8,128)} %fusion.7), channel_id=1, source_target_pairs={{0,28},{4,0},{8,4},{12,8},{16,12},{20,16},{24,20},{28,24},{1,29},{... | collective-permute-start | bytes 3145736 | tf_op jit(solution)/shard_map/ppermute | solution.py:14
  48.9 2.7 %collective-permute-start.3 = (f32[1024,256]{1,0:T(8,128)S(1)}, f32[1024,256]{1,0:T(8,128)S(1)}, u32[]{:S(2)}, u32[]{:S(2)}) collective-permute-start(f32[1024,256]{1,0:T(8,128)S(1)} %convolution_multiply_fusion.5), channel_id=1, source_target_pairs={{0,1},{1,0},{2,3},{3,2},{4,5},{5,4},{6,7},{7,6},{8,9},{9,8},{10,11... | collective-permute-start | bytes 3145736 | tf_op jit(solution)/shard_map/ppermute | solution.py:52
  52.7 25.5 %collective-permute-start.4 = (f32[1024,256]{1,0:T(8,128)}, f32[1024,256]{1,0:T(8,128)}, u32[]{:S(2)}, u32[]{:S(2)}) collective-permute-start(f32[1024,256]{1,0:T(8,128)} %add.63), channel_id=1, source_target_pairs={{0,2},{1,3},{2,0},{3,1},{4,6},{5,7},{6,4},{7,5},{8,10},{9,11},{10,... | collective-permute-start | bytes 3145736 | tf_op jit(solution)/shard_map/ppermute | solution.py:52
  55.0 27.8 %collective-permute-start.5 = (f32[1024,256]{1,0:T(8,128)}, f32[1024,256]{1,0:T(8,128)S(1)}, u32[]{:S(2)}, u32[]{:S(2)}) collective-permute-start(f32[1024,256]{1,0:T(8,128)} %fusion.6), channel_id=1, source_target_pairs={{0,28},{4,0},{8,4},{12,8},{16,12},{20,16},{24,20},{28,24},{1,29},{... | collective-permute-start | bytes 3145736 | tf_op jit(solution)/shard_map/ppermute | solution.py:14
  86.8 2.7 %collective-permute-start.6 = (f32[1024,256]{1,0:T(8,128)S(1)}, f32[1024,256]{1,0:T(8,128)S(1)}, u32[]{:S(2)}, u32[]{:S(2)}) collective-permute-start(f32[1024,256]{1,0:T(8,128)S(1)} %convolution_multiply_fusion.3), channel_id=1, source_target_pairs={{0,1},{1,0},{2,3},{3,2},{4,5},{5,4},{6,7},{7,6},{8,9},{9,8},{10,11... | collective-permute-start | bytes 3145736 | tf_op jit(solution)/shard_map/ppermute | solution.py:52
  90.6 25.5 %collective-permute-start.7 = (f32[1024,256]{1,0:T(8,128)}, f32[1024,256]{1,0:T(8,128)}, u32[]{:S(2)}, u32[]{:S(2)}) collective-permute-start(f32[1024,256]{1,0:T(8,128)} %add.68), channel_id=1, source_target_pairs={{0,2},{1,3},{2,0},{3,1},{4,6},{5,7},{6,4},{7,5},{8,10},{9,11},{10,... | collective-permute-start | bytes 3145736 | tf_op jit(solution)/shard_map/ppermute | solution.py:52
  93.9 27.8 %collective-permute-start.8 = (f32[1024,256]{1,0:T(8,128)}, f32[1024,256]{1,0:T(8,128)S(1)}, u32[]{:S(2)}, u32[]{:S(2)}) collective-permute-start(f32[1024,256]{1,0:T(8,128)} %fusion.5), channel_id=1, source_target_pairs={{0,28},{4,0},{8,4},{12,8},{16,12},{20,16},{24,20},{28,24},{1,29},{... | collective-permute-start | bytes 3145736 | tf_op jit(solution)/shard_map/ppermute | solution.py:14
  125.7 2.7 %collective-permute-start.9 = (f32[1024,256]{1,0:T(8,128)S(1)}, f32[1024,256]{1,0:T(8,128)S(1)}, u32[]{:S(2)}, u32[]{:S(2)}) collective-permute-start(f32[1024,256]{1,0:T(8,128)S(1)} %convolution_multiply_fusion.1), channel_id=1, source_target_pairs={{0,1},{1,0},{2,3},{3,2},{4,5},{5,4},{6,7},{7,6},{8,9},{9,8},{10,11... | collective-permute-start | bytes 3145736 | tf_op jit(solution)/shard_map/ppermute | solution.py:52
  126.6 49.9 %copy-start.1 = (f32[1024,256]{1,0:T(8,128)S(1)}, f32[1024,256]{1,0:T(8,128)}, u32[]{:S(2)}) copy-start(f32[1024,256]{1,0:T(8,128)} %get-tuple-element.3) | copy-start | bytes 3145732
  126.6 49.9 %collective-permute-start.11 = (f32[1024,256]{1,0:T(8,128)S(1)}, f32[1024,256]{1,0:T(8,128)S(1)}, u32[]{:S(2)}, u32[]{:S(2)}) collective-permute-start(f32[1024,256]{1,0:T(8,128)S(1)} %fusion.4), channel_id=1, source_target_pairs={{0,12},{4,16},{8,20},{12,24},{16,28},{20,0},{24,4},{28,8},{1,13},{... | collective-permute-start | bytes 3145736 | tf_op jit(solution)/shard_map/ppermute | solution.py:14
  128.6 47.9 %collective-permute-start.10 = (f32[1024,256]{1,0:T(8,128)S(1)}, f32[1024,256]{1,0:T(8,128)S(1)}, u32[]{:S(2)}, u32[]{:S(2)}) collective-permute-start(f32[1024,256]{1,0:T(8,128)S(1)} %add.73), channel_id=1, source_target_pairs={{0,2},{1,3},{2,0},{3,1},{4,6},{5,7},{6,4},{7,5},{8,10},{9,11},{10,... | collective-permute-start | bytes 3145736 | tf_op jit(solution)/shard_map/ppermute | solution.py:52
